TPU v7x, 128 devices: a whole 4x4x4 slice. The times are simulated.
128 devices in a mesh: slab: 16 (over x, y_hi, core), tile: 8 (over y_lo, z).
Axes of the slice: x: 4, y: 4 (y_hi: 2, y_lo: 2; y = y_hi * 2 + y_lo), z: 4, core: 2. Of those that a mesh axis runs over, the one named last changes fastest.
Arguments:
- velocity: float32 [3, 512, 128, 128], P(None, 'slab', 'tile'), may hold values from -4 to 4
- viscosity: float32 [512, 128, 128], P('slab', 'tile'), may hold values from 0.2 to 0.6
- basis: bfloat16 [32, 3, 512, 128, 128], P(None, None, ('slab', 'tile')), may hold values from -6 to 6
- sigma: float32 [32], replicated, may hold values from 0.3 to 3
- rotation: float32 [35, 32], replicated, may hold values from -1 to 1
Outputs:
- advanced: float32 [3, 512, 128, 128], P(None, 'slab', 'tile')
- r_factor: float32 [35, 35], replicated
- new_basis: bfloat16 [32, 3, 512, 128, 128], P(None, None, ('slab', 'tile'))
All inputs are finite; a program needn't handle non-finite values.
Results may differ from a plain program's by a relative error of at most 0.001.
Values sent between devices are 32-bit elements; how exact they have to be, the bound alone decides.
A program may use at most 256 MiB of HBM per device.

v0:
```python
import math
import jax
import jax.numpy as jnp
from jax import lax
from jax.sharding import PartitionSpec as P

step_size = 0.25


def extended(block, sides, width):
    for axis, dim in sides:
        count = lax.axis_size(axis)
        forward = [(i, i + 1) for i in range(count - 1)]
        forward.append((count - 1, 0))
        backward = [(target, source) for source, target in forward]
        low = lax.ppermute(
            lax.slice_in_dim(block, block.shape[dim] - width, None, axis=dim), axis, forward
        )
        high = lax.ppermute(lax.slice_in_dim(block, 0, width, axis=dim), axis, backward)
        block = jnp.concatenate([low, block, high], axis=dim)
    return block


def upper_factor(gram):
    order = gram.shape[0]
    positions = jnp.arange(order)
    factor = jnp.zeros_like(gram)
    for column_index in range(order):
        above = factor[:, column_index]
        remainder = gram[column_index] - jnp.dot(
            above, factor, precision=lax.Precision.HIGHEST, preferred_element_type=jnp.float32
        )
        pivot = jnp.sqrt(remainder[column_index])
        new_row = jnp.where(positions >= column_index, remainder / pivot, 0.0)
        factor = factor.at[column_index].set(new_row)
    return factor


def upper_solve(factor, right_hand):
    order = factor.shape[0]
    solved = jnp.zeros_like(right_hand)
    for row_index in range(order - 1, -1, -1):
        partial_sum = jnp.dot(
            factor[row_index],
            solved,
            precision=lax.Precision.HIGHEST,
            preferred_element_type=jnp.float32,
        )
        solved = solved.at[row_index].set(
            (right_hand[row_index] - partial_sum) / factor[row_index, row_index]
        )
    return solved


def advance(padded, viscosity):
    centre = padded[:, 1:-1, 1:-1, :]
    forward_x = padded[:, 2:, 1:-1, :]
    backward_x = padded[:, :-2, 1:-1, :]
    forward_z = padded[:, 1:-1, 2:, :]
    backward_z = padded[:, 1:-1, :-2, :]
    walled = jnp.pad(centre, ((0, 0), (0, 0), (0, 0), (1, 1)))
    above_y = walled[..., 2:]
    below_y = walled[..., :-2]
    laplace = forward_x + backward_x + forward_z + backward_z + above_y + below_y - 6.0 * centre
    carried = (
        centre[0:1] * (forward_x - backward_x)
        + centre[1:2] * (above_y - below_y)
        + centre[2:3] * (forward_z - backward_z)
    )
    return centre + step_size * (viscosity * laplace - 0.5 * carried)


def shards(velocity, viscosity, basis, sigma, rotation):
    current = velocity
    history = [velocity]
    for repeat in range(2):
        padded = extended(current, (("slab", 1), ("tile", 2)), 1)
        current = advance(padded, viscosity)
        history.append(current)
    snapshots = lax.all_to_all(jnp.stack(history), "tile", split_axis=2, concat_axis=3, tiled=True)
    strip_width = basis.shape[2]
    row_count = (
        3
        * strip_width
        * lax.axis_size("slab")
        * lax.axis_size("tile")
        * basis.shape[3]
        * basis.shape[4]
    )
    row_scale = math.sqrt(row_count)
    width_all = sigma.shape[0] + 3
    scaled = basis.astype(jnp.float32) * sigma[:, None, None, None, None]
    columns = jnp.concatenate([scaled, snapshots], 0).reshape(width_all, -1)
    local_gram = jnp.dot(
        columns, columns.T, precision=lax.Precision.HIGHEST, preferred_element_type=jnp.float32
    )
    gram = lax.psum(local_gram, ("slab", "tile"))
    factor = upper_factor(gram)
    mixing = upper_solve(factor, rotation) * row_scale
    rotated = jnp.dot(
        mixing.T, columns, precision=lax.Precision.HIGHEST, preferred_element_type=jnp.float32
    )
    rotated = rotated.reshape(basis.shape).astype(jnp.bfloat16)
    return (current, factor / row_scale, rotated)


def solution(mesh):
    in_specs = (
        P(None, "slab", "tile", None),
        P("slab", "tile", None),
        P(None, None, ("slab", "tile"), None, None),
        P(),
        P(),
    )
    out_specs = (P(None, "slab", "tile", None), P(), P(None, None, ("slab", "tile"), None, None))
    return jax.shard_map(shards, mesh=mesh, in_specs=in_specs, out_specs=out_specs, check_vma=False)
```

profile of v0, /device:TPU:1, one launch (start us, length us, event | category | flops | bytes accessed | tf_op | source)
XLA Modules:
  0.0 461.0 jit_solution(1416673244914366114)
XLA Ops:
  1.4 4.3 collective-permute-start.1
  6.7 1.2 copy_bitcast_fusion.1
  7.9 2.6 collective-permute-done
  10.5 3.9 collective-permute-start.2
  14.5 1.2 slice_bitcast_fusion.5
  15.6 1.2 copy.42
  16.8 2.7 collective-permute-done.3
  19.6 1.8 multiply_add_fusion.1
  21.4 3.4 collective-permute-start.5
  25.7 4.1 collective-permute-done.4
  30.0 1.5 collective-permute-start.7
  31.5 1.4 collective-permute-done.6
  32.9 2.2 collective-permute-done.7
  35.1 1.8 fusion.306
  36.9 1.6 pad_maximum_fusion.1
  38.6 3.8 all-to-all-start
  42.4 11.8 %convert_multiply_fusion = f32[32,3,4,128,128]{4,0,3,2,1:T(8,128)S(1)} fusion(bf16[32,3,4,128,128]{4,3,2,1,0:T(8,128)(2,1)} %param.147, f32[32]{0:T(128)} %param.148), kind=kLoop, calls=%fused_computation.8 | loop fusion | flops 12582912 | bytes 37748864 | tf_op jit(solution)/shard_map/mul | solution.py:92
  54.1 28.1 %copy.82 = f32[32,3,4,128,128]{4,3,2,1,0:T(8,128)} copy(f32[32,3,4,128,128]{4,0,3,2,1:T(8,128)S(1)} %convert_multiply_fusion) | data formatting | bytes 50331648 | tf_op jit(solution)/shard_map/mul | solution.py:92
  82.3 25.1 %copy.100 = f32[4,8,1536,128]{3,1,2,0:T(8,128)} copy(f32[4,8,1536,128]{3,2,1,0:T(8,128)} %bitcast.1128) | data formatting | bytes 50331648
  107.4 1.0 slice_reduce_fusion.35
  108.5 1.1 slice_reduce_fusion.34
  110.7 0.9 copy.84
  111.6 1.4 copy-done.3
  113.0 3.0 copy.46
  116.0 28.8 %fusion.9 = f32[35,35]{1,0:T(8,128)S(1)} fusion(f32[3,3,4,128,128]{4,0,3,2,1:T(4,128)S(1)} %bitcast.1130, f32[32,3,4,128,128]{4,0,3,2,1:T(8,128)} %copy-done.1), kind=kOutput, calls=%fused_computation.15 | convolution fusion | flops 2897018880 | bytes 27530020 | tf_op jit(solution)/shard_map/dot_general | solution.py:94
  144.8 68.9 %psum.7 = f32[35,35]{1,0:T(8,128)S(1)} all-reduce(f32[35,35]{1,0:T(8,128)S(1)} %fusion.9), channel_id=1, replica_groups=mesh['slab'=16,'tile'=8] {'slab','tile'}, use_global_device_ids=true, to_apply=%region_0.1 | all-reduce | flops 1225 | bytes 9800 | tf_op jit(solution)/shard_map/psum | solution.py:97
  298.0 1.4 fusion.87
  299.7 1.5 fusion.89
  301.4 1.4 fusion.91
  303.0 1.4 fusion.93
  304.7 1.4 fusion.95
  306.4 1.4 fusion.97
  308.1 1.5 fusion.99
  309.9 1.4 fusion.101
  311.6 1.4 fusion.103
  313.2 1.5 fusion.105
  315.0 1.4 fusion.107
  316.6 1.5 fusion.109
  318.3 1.4 fusion.111
  320.0 1.4 fusion.113
  321.7 1.4 fusion.115
  323.3 1.5 fusion.117
  325.1 1.4 fusion.119
  326.7 1.4 fusion.121
  328.4 1.4 fusion.123
  330.0 1.4 fusion.125
  331.7 1.5 fusion.127
  333.4 1.5 fusion.129
  335.2 1.4 fusion.131
  336.8 1.5 fusion.133
  338.6 1.4 fusion.135
  340.3 1.4 fusion.137
  342.0 1.4 fusion.139
  343.7 1.4 fusion.141
  345.3 1.5 fusion.143
  347.0 1.4 fusion.145
  348.6 1.4 fusion.147
  350.3 1.4 fusion.149
  352.0 1.4 fusion.151
  353.6 10.1 %pad_maximum_fusion = f32[35,196608]{1,0:T(8,128)S(1)} fusion(f32[3,196608]{1,0:T(4,128)S(1)} %bitcast.1131, f32[32,196608]{1,0:T(8,128)} %bitcast.1127), kind=kLoop, calls=%fused_computation.4 | loop fusion | flops 6881280 | bytes 55050240 | tf_op jit(solution)/shard_map/concatenate | solution.py:93
  363.7 14.4 %copy.89 = f32[5,8,1536,128]{3,2,1,0:T(8,128)} copy(f32[5,8,1536,128]{3,1,2,0:T(8,128)S(1)} %bitcast.1125) | data formatting | bytes 62914560
  378.1 20.3 %slice.2142 = f32[35,1536,128]{2,1,0:T(8,128)} slice(f32[40,1536,128]{2,1,0:T(8,128)} %bitcast.1126), slice={[0:35], [0:1536], [0:128]} | slice | bytes 55050240
  398.3 48.0 %fusion.6 = bf16[32,3,4,128,128]{4,0,3,2,1:T(8,128)(2,1)S(1)} fusion(f32[3,4,128,128,35]{3,2,1,0,4:T(8,128)} %bitcast.1124, f32[35,32]{0,1:T(8,128)S(1)} %scatter.349), kind=kOutput, calls=%fused_computation.9 | convolution fusion | flops 2648704000 | bytes 40112512 | tf_op jit(solution)/shard_map/dot_general | solution.py:100
  446.4 14.5 %copy.85 = bf16[32,3,4,128,128]{4,3,2,1,0:T(8,128)(2,1)} copy(bf16[32,3,4,128,128]{4,0,3,2,1:T(8,128)(2,1)S(1)} %fusion.6) | data formatting | bytes 25165824
  (336 shorter events, 71.9 us)
Async XLA Ops:
  1.4 5.3 %collective-permute-start.1 = (f32[3,1,16,128]{3,2,0,1:T(8,128)S(1)}, f32[3,1,16,128]{3,2,0,1:T(8,128)S(1)}, u32[]{:S(2)}, u32[]{:S(2)}) collective-permute-start(f32[3,1,16,128]{3,2,0,1:T(8,128)S(1)} %get-tuple-element.905), channel_id=1, source_target_pairs={{0,8},{8,16},{16,24},{24,32},{32,40},{40,48},{48,56},{56,64},{64,7... | collective-permute-start | bytes 73736 | tf_op jit(solution)/shard_map/ppermute | solution.py:16
  5.7 4.8 %collective-permute-start = (f32[3,1,16,128]{3,2,0,1:T(8,128)S(1)}, f32[3,1,16,128]{3,2,0,1:T(8,128)S(1)}, u32[]{:S(2)}, u32[]{:S(2)}) collective-permute-start(f32[3,1,16,128]{3,2,0,1:T(8,128)S(1)} %get-tuple-element.904), channel_id=1, source_target_pairs={{8,0},{16,8},{24,16},{32,24},{40,32},{48,40},{56,48},{64,56},{72,6... | collective-permute-start | bytes 73736 | tf_op jit(solution)/shard_map/ppermute | solution.py:19
  10.5 6.3 %collective-permute-start.2 = (f32[3,34,1,128]{3,2,0,1:T(1,128)S(1)}, f32[3,34,1,128]{3,2,0,1:T(1,128)S(1)}, u32[]{:S(2)}, u32[]{:S(2)}) collective-permute-start(f32[3,34,1,128]{3,2,0,1:T(1,128)S(1)} %get-tuple-element.892), channel_id=1, source_target_pairs={{1,0},{2,1},{3,2},{4,3},{5,4},{6,5},{7,6},{0,7},{9,8},{10,9},{11,1... | collective-permute-start | bytes 156680 | tf_op jit(solution)/shard_map/ppermute | solution.py:19
  14.5 5.1 %collective-permute-start.3 = (f32[3,34,1,128]{3,2,0,1:T(1,128)S(1)}, f32[3,34,1,128]{3,2,0,1:T(1,128)S(1)}, u32[]{:S(2)}, u32[]{:S(2)}) collective-permute-start(f32[3,34,1,128]{3,2,0,1:T(1,128)S(1)} %get-tuple-element.893), channel_id=1, source_target_pairs={{0,1},{1,2},{2,3},{3,4},{4,5},{5,6},{6,7},{7,0},{8,9},{9,10},{10,1... | collective-permute-start | bytes 156680 | tf_op jit(solution)/shard_map/ppermute | solution.py:16
  21.4 4.3 collective-permute-start.5
  24.8 5.1 %collective-permute-start.4 = (f32[3,1,16,128]{3,2,0,1:T(8,128)S(1)}, f32[3,1,16,128]{3,2,0,1:T(8,128)S(1)}, u32[]{:S(2)}, u32[]{:S(2)}) collective-permute-start(f32[3,1,16,128]{3,2,0,1:T(8,128)S(1)} %get-tuple-element.900), channel_id=1, source_target_pairs={{8,0},{16,8},{24,16},{32,24},{40,32},{48,40},{56,48},{64,56},{72,6... | collective-permute-start | bytes 73736 | tf_op jit(solution)/shard_map/ppermute | solution.py:19
  29.9 3.0 collective-permute-start.6
  30.0 5.2 %collective-permute-start.7 = (f32[3,34,1,128]{3,2,0,1:T(1,128)S(1)}, f32[3,34,1,128]{3,2,0,1:T(1,128)S(1)}, u32[]{:S(2)}, u32[]{:S(2)}) collective-permute-start(f32[3,34,1,128]{3,2,0,1:T(1,128)S(1)} %get-tuple-element.891), channel_id=1, source_target_pairs={{0,1},{1,2},{2,3},{3,4},{4,5},{5,6},{6,7},{7,0},{8,9},{9,10},{10,1... | collective-permute-start | bytes 156680 | tf_op jit(solution)/shard_map/ppermute | solution.py:16
  31.5 7.0 %copy-start.4 = (f32[32,16,128]{2,1,0:T(8,128)}, f32[32,16,128]{2,1,0:T(8,128)S(1)}, u32[]{:S(2)}) copy-start(f32[32,16,128]{2,1,0:T(8,128)S(1)} %get-tuple-element.897) | copy-start | bytes 786436
  31.5 7.0 %copy-start.6 = (f32[32,16,128]{2,1,0:T(8,128)}, f32[32,16,128]{2,1,0:T(8,128)S(1)}, u32[]{:S(2)}) copy-start(f32[32,16,128]{2,1,0:T(8,128)S(1)} %get-tuple-element.898) | copy-start | bytes 786436
  35.1 3.4 copy-start.10
  38.6 73.0 %all-to-all-start = ((f32[3,3,32,16,128]{4,3,1,0,2:T(8,128)}), f32[3,3,32,16,128]{4,3,1,0,2:T(8,128)S(1)}, u32[]{:S(2)}, u32[]{:S(2)}) async-start(f32[3,3,32,16,128]{4,3,1,0,2:T(8,128)} %pad_maximum_fusion.1), calls=%async_computation | async-start | bytes 4718592 | tf_op jit(solution)/shard_map/all_to_all | solution.py:80
  54.1 28.2 %copy-start.1 = (f32[32,3,4,128,128]{4,0,3,2,1:T(8,128)}, f32[32,3,4,128,128]{4,0,3,2,1:T(8,128)S(1)}, u32[]{:S(2)}) copy-start(f32[32,3,4,128,128]{4,0,3,2,1:T(8,128)S(1)} %convert_multiply_fusion) | copy-start | bytes 75497472
  82.3 25.1 %copy-start.2 = (f32[35,32]{0,1:T(8,128)S(1)}, f32[35,32]{0,1:T(8,128)}, u32[]{:S(2)}) copy-start(f32[35,32]{0,1:T(8,128)} %param.149) | copy-start | bytes 13444
  82.3 27.3 %copy-start.5 = (f32[32,16,128]{2,1,0:T(8,128)S(1)}, f32[32,16,128]{2,1,0:T(8,128)}, u32[]{:S(2)}) copy-start(f32[32,16,128]{2,1,0:T(8,128)} %copy-done.4) | copy-start | bytes 786436
  82.3 27.3 %copy-start.7 = (f32[32,16,128]{2,1,0:T(8,128)S(1)}, f32[32,16,128]{2,1,0:T(8,128)}, u32[]{:S(2)}) copy-start(f32[32,16,128]{2,1,0:T(8,128)} %copy-done.6) | copy-start | bytes 786436
  82.3 27.2 %copy-start.8 = (f32[32,16,128]{2,1,0:T(8,128)S(1)}, f32[32,16,128]{2,1,0:T(8,128)}, u32[]{:S(2)}) copy-start(f32[32,16,128]{2,1,0:T(8,128)} %param.146) | copy-start | bytes 786436
  82.3 27.2 %copy-start.11 = (f32[3,34,1,128]{3,2,0,1:T(1,128)S(1)}, f32[3,34,1,128]{3,2,0,1:T(1,128)}, u32[]{:S(2)}) copy-start(f32[3,34,1,128]{3,2,0,1:T(1,128)} %copy-done.10) | copy-start | bytes 156676
  110.4 185.6 %copy-start.35 = (f32[32]{0:T(128)S(1)}, f32[32]{0:T(128)}, u32[]{:S(2)}) copy-start(f32[32]{0:T(128)} %get-tuple-element.889) | copy-start | bytes 388
  110.4 186.4 %copy-start.30 = (f32[32]{0:T(128)S(1)}, f32[32]{0:T(128)}, u32[]{:S(2)}) copy-start(f32[32]{0:T(128)} %get-tuple-element.888) | copy-start | bytes 388
  110.4 187.5 %copy-start.29 = (f32[32]{0:T(128)S(1)}, f32[32]{0:T(128)}, u32[]{:S(2)}) copy-start(f32[32]{0:T(128)} %get-tuple-element.887) | copy-start | bytes 388
  110.4 189.2 %copy-start.34 = (f32[32]{0:T(128)S(1)}, f32[32]{0:T(128)}, u32[]{:S(2)}) copy-start(f32[32]{0:T(128)} %get-tuple-element.886) | copy-start | bytes 388
  110.5 191.0 %copy-start.28 = (f32[32]{0:T(128)S(1)}, f32[32]{0:T(128)}, u32[]{:S(2)}) copy-start(f32[32]{0:T(128)} %get-tuple-element.885) | copy-start | bytes 388
  110.5 192.6 %copy-start.27 = (f32[32]{0:T(128)S(1)}, f32[32]{0:T(128)}, u32[]{:S(2)}) copy-start(f32[32]{0:T(128)} %get-tuple-element.884) | copy-start | bytes 388
  110.5 194.3 %copy-start.26 = (f32[32]{0:T(128)S(1)}, f32[32]{0:T(128)}, u32[]{:S(2)}) copy-start(f32[32]{0:T(128)} %get-tuple-element.883) | copy-start | bytes 388
  110.5 196.0 %copy-start.25 = (f32[32]{0:T(128)S(1)}, f32[32]{0:T(128)}, u32[]{:S(2)}) copy-start(f32[32]{0:T(128)} %get-tuple-element.882) | copy-start | bytes 388
  110.5 197.6 %copy-start.24 = (f32[32]{0:T(128)S(1)}, f32[32]{0:T(128)}, u32[]{:S(2)}) copy-start(f32[32]{0:T(128)} %get-tuple-element.881) | copy-start | bytes 388
  110.5 199.4 %copy-start.23 = (f32[32]{0:T(128)S(1)}, f32[32]{0:T(128)}, u32[]{:S(2)}) copy-start(f32[32]{0:T(128)} %get-tuple-element.880) | copy-start | bytes 388
  110.5 201.1 %copy-start.22 = (f32[32]{0:T(128)S(1)}, f32[32]{0:T(128)}, u32[]{:S(2)}) copy-start(f32[32]{0:T(128)} %get-tuple-element.879) | copy-start | bytes 388
  110.5 202.7 %copy-start.33 = (f32[32]{0:T(128)S(1)}, f32[32]{0:T(128)}, u32[]{:S(2)}) copy-start(f32[32]{0:T(128)} %get-tuple-element.878) | copy-start | bytes 388
  110.5 204.4 %copy-start.21 = (f32[32]{0:T(128)S(1)}, f32[32]{0:T(128)}, u32[]{:S(2)}) copy-start(f32[32]{0:T(128)} %get-tuple-element.877) | copy-start | bytes 388
  110.5 206.1 %copy-start.20 = (f32[32]{0:T(128)S(1)}, f32[32]{0:T(128)}, u32[]{:S(2)}) copy-start(f32[32]{0:T(128)} %get-tuple-element.876) | copy-start | bytes 388
  110.6 207.8 %copy-start.19 = (f32[32]{0:T(128)S(1)}, f32[32]{0:T(128)}, u32[]{:S(2)}) copy-start(f32[32]{0:T(128)} %get-tuple-element.875) | copy-start | bytes 388
  110.6 209.5 %copy-start.18 = (f32[32]{0:T(128)S(1)}, f32[32]{0:T(128)}, u32[]{:S(2)}) copy-start(f32[32]{0:T(128)} %get-tuple-element.873) | copy-start | bytes 388
  110.6 211.1 %copy-start.17 = (f32[32]{0:T(128)S(1)}, f32[32]{0:T(128)}, u32[]{:S(2)}) copy-start(f32[32]{0:T(128)} %get-tuple-element.872) | copy-start | bytes 388
  110.6 212.8 %copy-start.16 = (f32[32]{0:T(128)S(1)}, f32[32]{0:T(128)}, u32[]{:S(2)}) copy-start(f32[32]{0:T(128)} %get-tuple-element.871) | copy-start | bytes 388
  110.6 214.5 %copy-start.15 = (f32[32]{0:T(128)S(1)}, f32[32]{0:T(128)}, u32[]{:S(2)}) copy-start(f32[32]{0:T(128)} %get-tuple-element.870) | copy-start | bytes 388
  110.6 216.1 %copy-start.32 = (f32[32]{0:T(128)S(1)}, f32[32]{0:T(128)}, u32[]{:S(2)}) copy-start(f32[32]{0:T(128)} %get-tuple-element.869) | copy-start | bytes 388
  110.6 217.8 %copy-start.14 = (f32[32]{0:T(128)S(1)}, f32[32]{0:T(128)}, u32[]{:S(2)}) copy-start(f32[32]{0:T(128)} %get-tuple-element.868) | copy-start | bytes 388
  110.6 219.4 %copy-start.13 = (f32[32]{0:T(128)S(1)}, f32[32]{0:T(128)}, u32[]{:S(2)}) copy-start(f32[32]{0:T(128)} %get-tuple-element.867) | copy-start | bytes 388
  110.6 221.0 %copy-start.12 = (f32[32]{0:T(128)S(1)}, f32[32]{0:T(128)}, u32[]{:S(2)}) copy-start(f32[32]{0:T(128)} %get-tuple-element.866) | copy-start | bytes 388
  110.6 229.6 %copy-start.31 = (f32[32]{0:T(128)S(1)}, f32[32]{0:T(128)}, u32[]{:S(2)}) copy-start(f32[32]{0:T(128)} %get-tuple-element.861) | copy-start | bytes 388
  111.6 1.4 copy-start.3
  213.8 2.1 copy-start.9
  293.9 4.0 copy-start
where the time goes:
time: 469 us; the launch traced here: 461 us
  local copies, waits for them, and re-layouts  153 us (33%)
  matrix products  153 us (33%)
  blocking collectives  68.9 us (15%)
  other arithmetic  28.8 us (6%)
  between operations  25.7 us (5%)
  starting transfers between devices  16.9 us (4%)
  waiting for transfers between devices  14.9 us (3%)
    unnamed x79, local copies, waits for them, and re-layouts  77.9 us
    psum x1, blocking collectives, shards(): gram = lax.psum(local_gram, ('slab', 'tile'))  68.9 us
    dot_general x35, matrix products, upper_solve(): jnp.dot(factor[row_index], solved, precision=lax.Precision.HIGHEST, prefe...  48.9 us
    dot_general x1, matrix products, shards(): jnp.dot(mixing.T, columns, precision=lax.Precision.HIGHEST, preferred_ele...  48 us
    dot_general x1, matrix products, shards(): jnp.dot(columns, columns.T, precision=lax.Precision.HIGHEST, preferred_el...  28.8 us
    mul x1, local copies, waits for them, and re-layouts, shards(): scaled = basis.astype(jnp.float32) * sigma[:, None, None, None, None]  28.1 us
    dot_general x35, matrix products, upper_factor(): jnp.dot(above, factor, precision=lax.Precision.HIGHEST, preferred_element...  27.4 us
    slice x34, local copies, waits for them, and re-layouts, upper_factor(): pivot = jnp.sqrt(remainder[column_index])  20.3 us
  transfers between devices with their start and end apart: 9, of which 7 were waited for; matrix products, arithmetic and copies ran while one was open for 16% of the time, Pallas kernels for 0%

commit v1 on v0

--- a/solution.py
+++ b/solution.py
@@ -94,7 +94,7 @@
     local_gram = jnp.dot(
         columns, columns.T, precision=lax.Precision.HIGHEST, preferred_element_type=jnp.float32
     )
-    gram = lax.psum(local_gram, ("slab", "tile"))
+    gram = lax.psum(lax.psum(local_gram, "tile"), "slab")
     factor = upper_factor(gram)
     mixing = upper_solve(factor, rotation) * row_scale
     rotated = jnp.dot(

time: 469 us -> 501 us (1.068)
  the two profiles are of different devices: /device:TPU:1 before, /device:TPU:0 now
where the time goes in v1:
time: 501 us; the launch traced here: 493 us
  local copies, waits for them, and re-layouts  153 us (31%)
  matrix products  153 us (31%)
  blocking collectives  99.5 us (20%)
  other arithmetic  28.8 us (6%)
  between operations  25.7 us (5%)
  starting transfers between devices  21.9 us (4%)
  waiting for transfers between devices  11.3 us (2%)
    psum x2, blocking collectives, shards(): gram = lax.psum(lax.psum(local_gram, 'tile'), 'slab')  99.5 us
    unnamed x79, local copies, waits for them, and re-layouts  77.9 us
    dot_general x35, matrix products, upper_solve(): jnp.dot(factor[row_index], solved, precision=lax.Precision.HIGHEST, prefe...  48.9 us
    dot_general x1, matrix products, shards(): jnp.dot(mixing.T, columns, precision=lax.Precision.HIGHEST, preferred_ele...  48 us
    dot_general x1, matrix products, shards(): jnp.dot(columns, columns.T, precision=lax.Precision.HIGHEST, preferred_el...  28.8 us
    mul x1, local copies, waits for them, and re-layouts, shards(): scaled = basis.astype(jnp.float32) * sigma[:, None, None, None, None]  28.1 us
    dot_general x35, matrix products, upper_factor(): jnp.dot(above, factor, precision=lax.Precision.HIGHEST, preferred_element...  27.4 us
    slice x34, local copies, waits for them, and re-layouts, upper_factor(): pivot = jnp.sqrt(remainder[column_index])  20.3 us
  transfers between devices with their start and end apart: 9, of which 5 were waited for; matrix products, arithmetic and copies ran while one was open for 15% of the time, Pallas kernels for 0%

profile of v1, /device:TPU:0, one launch (start us, length us, event | category | flops | bytes accessed | tf_op | source)
XLA Modules:
  0.0 493.0 jit_solution(269705700645699836)
XLA Ops:
  1.4 5.4 %collective-permute-start = (f32[3,1,16,128]{3,2,0,1:T(8,128)S(1)}, f32[3,1,16,128]{3,2,0,1:T(8,128)S(1)}, u32[]{:S(2)}, u32[]{:S(2)}) collective-permute-start(f32[3,1,16,128]{3,2,0,1:T(8,128)S(1)} %get-tuple-element.904), channel_id=1, source_target_pairs={{8,0},{16,8},{24,16},{32,24},{40,32},{48,40},{56,48},{64,56},{72,6... | collective-permute-start | bytes 73736 | tf_op jit(solution)/shard_map/ppermute | solution.py:19
  6.8 1.5 collective-permute-done.1
  8.3 1.2 copy_bitcast_fusion.1
  9.6 5.2 %collective-permute-start.2 = (f32[3,34,1,128]{3,2,0,1:T(1,128)S(1)}, f32[3,34,1,128]{3,2,0,1:T(1,128)S(1)}, u32[]{:S(2)}, u32[]{:S(2)}) collective-permute-start(f32[3,34,1,128]{3,2,0,1:T(1,128)S(1)} %get-tuple-element.892), channel_id=1, source_target_pairs={{1,0},{2,1},{3,2},{4,3},{5,4},{6,5},{7,6},{0,7},{9,8},{10,9},{11,1... | collective-permute-start | bytes 156680 | tf_op jit(solution)/shard_map/ppermute | solution.py:19
  14.8 1.2 slice_bitcast_fusion.5
  16.0 1.2 copy.42
  17.2 3.9 collective-permute-done.3
  21.0 1.8 multiply_add_fusion.1
  23.0 5.3 %collective-permute-start.4 = (f32[3,1,16,128]{3,2,0,1:T(8,128)S(1)}, f32[3,1,16,128]{3,2,0,1:T(8,128)S(1)}, u32[]{:S(2)}, u32[]{:S(2)}) collective-permute-start(f32[3,1,16,128]{3,2,0,1:T(8,128)S(1)} %get-tuple-element.900), channel_id=1, source_target_pairs={{8,0},{16,8},{24,16},{32,24},{40,32},{48,40},{56,48},{64,56},{72,6... | collective-permute-start | bytes 73736 | tf_op jit(solution)/shard_map/ppermute | solution.py:19
  28.3 1.5 collective-permute-done.5
  30.3 1.7 collective-permute-start.7
  32.1 2.0 collective-permute-done.6
  34.1 2.4 collective-permute-done.7
  36.5 1.8 fusion.306
  38.3 1.6 pad_maximum_fusion.1
  39.9 3.8 all-to-all-start
  43.7 11.8 %convert_multiply_fusion = f32[32,3,4,128,128]{4,0,3,2,1:T(8,128)S(1)} fusion(bf16[32,3,4,128,128]{4,3,2,1,0:T(8,128)(2,1)} %param.147, f32[32]{0:T(128)} %param.148), kind=kLoop, calls=%fused_computation.8 | loop fusion | flops 12582912 | bytes 37748864 | tf_op jit(solution)/shard_map/mul | solution.py:92
  55.5 28.1 %copy.82 = f32[32,3,4,128,128]{4,3,2,1,0:T(8,128)} copy(f32[32,3,4,128,128]{4,0,3,2,1:T(8,128)S(1)} %convert_multiply_fusion) | data formatting | bytes 50331648 | tf_op jit(solution)/shard_map/mul | solution.py:92
  83.7 25.1 %copy.100 = f32[4,8,1536,128]{3,1,2,0:T(8,128)} copy(f32[4,8,1536,128]{3,2,1,0:T(8,128)} %bitcast.1128) | data formatting | bytes 50331648
  108.8 1.0 slice_reduce_fusion.35
  109.8 1.1 slice_reduce_fusion.34
  113.0 1.4 copy-done.3
  114.4 3.0 copy.46
  117.4 28.8 %fusion.9 = f32[35,35]{1,0:T(8,128)S(1)} fusion(f32[3,3,4,128,128]{4,0,3,2,1:T(4,128)S(1)} %bitcast.1130, f32[32,3,4,128,128]{4,0,3,2,1:T(8,128)} %copy-done.1), kind=kOutput, calls=%fused_computation.15 | convolution fusion | flops 2897018880 | bytes 27530020 | tf_op jit(solution)/shard_map/dot_general | solution.py:94
  146.2 34.6 %psum.14 = f32[35,35]{1,0:T(8,128)S(1)} all-reduce(f32[35,35]{1,0:T(8,128)S(1)} %fusion.9), channel_id=1, replica_groups=mesh['slab'=16,'tile'=8] {'tile'}, use_global_device_ids=true, to_apply=%region_0.1 | all-reduce | flops 1225 | bytes 9800 | tf_op jit(solution)/shard_map/psum | solution.py:97
  180.8 64.9 %psum.15 = f32[35,35]{1,0:T(8,128)S(1)} all-reduce(f32[35,35]{1,0:T(8,128)S(1)} %psum.14), channel_id=1, replica_groups=mesh['slab'=16,'tile'=8] {'slab'}, use_global_device_ids=true, to_apply=%region_1.2 | all-reduce | flops 1225 | bytes 9800 | tf_op jit(solution)/shard_map/psum | solution.py:97
  329.9 1.4 fusion.87
  331.6 1.5 fusion.89
  333.4 1.4 fusion.91
  335.0 1.4 fusion.93
  336.7 1.4 fusion.95
  338.4 1.4 fusion.97
  340.1 1.5 fusion.99
  341.8 1.4 fusion.101
  343.5 1.4 fusion.103
  345.2 1.5 fusion.105
  346.9 1.4 fusion.107
  348.6 1.5 fusion.109
  350.3 1.4 fusion.111
  352.0 1.4 fusion.113
  353.6 1.4 fusion.115
  355.3 1.5 fusion.117
  357.0 1.4 fusion.119
  358.6 1.4 fusion.121
  360.3 1.4 fusion.123
  362.0 1.4 fusion.125
  363.6 1.5 fusion.127
  365.3 1.5 fusion.129
  367.1 1.4 fusion.131
  368.8 1.5 fusion.133
  370.5 1.4 fusion.135
  372.2 1.4 fusion.137
  373.9 1.4 fusion.139
  375.6 1.4 fusion.141
  377.2 1.5 fusion.143
  378.9 1.4 fusion.145
  380.6 1.4 fusion.147
  382.3 1.4 fusion.149
  383.9 1.4 fusion.151
  385.5 10.1 %pad_maximum_fusion = f32[35,196608]{1,0:T(8,128)S(1)} fusion(f32[3,196608]{1,0:T(4,128)S(1)} %bitcast.1131, f32[32,196608]{1,0:T(8,128)} %bitcast.1127), kind=kLoop, calls=%fused_computation.4 | loop fusion | flops 6881280 | bytes 55050240 | tf_op jit(solution)/shard_map/concatenate | solution.py:93
  395.6 14.4 %copy.89 = f32[5,8,1536,128]{3,2,1,0:T(8,128)} copy(f32[5,8,1536,128]{3,1,2,0:T(8,128)S(1)} %bitcast.1125) | data formatting | bytes 62914560
  410.0 20.3 %slice.2142 = f32[35,1536,128]{2,1,0:T(8,128)} slice(f32[40,1536,128]{2,1,0:T(8,128)} %bitcast.1126), slice={[0:35], [0:1536], [0:128]} | slice | bytes 55050240
  430.3 48.0 %fusion.6 = bf16[32,3,4,128,128]{4,0,3,2,1:T(8,128)(2,1)S(1)} fusion(f32[3,4,128,128,35]{3,2,1,0,4:T(8,128)} %bitcast.1124, f32[35,32]{0,1:T(8,128)S(1)} %scatter.349), kind=kOutput, calls=%fused_computation.9 | convolution fusion | flops 2648704000 | bytes 40112512 | tf_op jit(solution)/shard_map/dot_general | solution.py:100
  478.3 14.5 %copy.85 = bf16[32,3,4,128,128]{4,3,2,1,0:T(8,128)(2,1)} copy(bf16[32,3,4,128,128]{4,0,3,2,1:T(8,128)(2,1)S(1)} %fusion.6) | data formatting | bytes 25165824
  (337 shorter events, 71.3 us)
Async XLA Ops:
  1.4 6.9 %collective-permute-start.1 = (f32[3,1,16,128]{3,2,0,1:T(8,128)S(1)}, f32[3,1,16,128]{3,2,0,1:T(8,128)S(1)}, u32[]{:S(2)}, u32[]{:S(2)}) collective-permute-start(f32[3,1,16,128]{3,2,0,1:T(8,128)S(1)} %get-tuple-element.905), channel_id=1, source_target_pairs={{0,8},{8,16},{16,24},{24,32},{32,40},{40,48},{48,56},{56,64},{64,7... | collective-permute-start | bytes 73736 | tf_op jit(solution)/shard_map/ppermute | solution.py:16
  1.4 8.1 %collective-permute-start = (f32[3,1,16,128]{3,2,0,1:T(8,128)S(1)}, f32[3,1,16,128]{3,2,0,1:T(8,128)S(1)}, u32[]{:S(2)}, u32[]{:S(2)}) collective-permute-start(f32[3,1,16,128]{3,2,0,1:T(8,128)S(1)} %get-tuple-element.904), channel_id=1, source_target_pairs={{8,0},{16,8},{24,16},{32,24},{40,32},{48,40},{56,48},{64,56},{72,6... | collective-permute-start | bytes 73736 | tf_op jit(solution)/shard_map/ppermute | solution.py:19
  9.6 7.6 %collective-permute-start.2 = (f32[3,34,1,128]{3,2,0,1:T(1,128)S(1)}, f32[3,34,1,128]{3,2,0,1:T(1,128)S(1)}, u32[]{:S(2)}, u32[]{:S(2)}) collective-permute-start(f32[3,34,1,128]{3,2,0,1:T(1,128)S(1)} %get-tuple-element.892), channel_id=1, source_target_pairs={{1,0},{2,1},{3,2},{4,3},{5,4},{6,5},{7,6},{0,7},{9,8},{10,9},{11,1... | collective-permute-start | bytes 156680 | tf_op jit(solution)/shard_map/ppermute | solution.py:19
  14.8 6.2 %collective-permute-start.3 = (f32[3,34,1,128]{3,2,0,1:T(1,128)S(1)}, f32[3,34,1,128]{3,2,0,1:T(1,128)S(1)}, u32[]{:S(2)}, u32[]{:S(2)}) collective-permute-start(f32[3,34,1,128]{3,2,0,1:T(1,128)S(1)} %get-tuple-element.893), channel_id=1, source_target_pairs={{0,1},{1,2},{2,3},{3,4},{4,5},{5,6},{6,7},{7,0},{8,9},{9,10},{10,1... | collective-permute-start | bytes 156680 | tf_op jit(solution)/shard_map/ppermute | solution.py:16
  22.9 6.9 %collective-permute-start.5 = (f32[3,1,16,128]{3,2,0,1:T(8,128)S(1)}, f32[3,1,16,128]{3,2,0,1:T(8,128)S(1)}, u32[]{:S(2)}, u32[]{:S(2)}) collective-permute-start(f32[3,1,16,128]{3,2,0,1:T(8,128)S(1)} %get-tuple-element.899), channel_id=1, source_target_pairs={{0,8},{8,16},{16,24},{24,32},{32,40},{40,48},{48,56},{56,64},{64,7... | collective-permute-start | bytes 73736 | tf_op jit(solution)/shard_map/ppermute | solution.py:16
  23.0 6.9 %collective-permute-start.4 = (f32[3,1,16,128]{3,2,0,1:T(8,128)S(1)}, f32[3,1,16,128]{3,2,0,1:T(8,128)S(1)}, u32[]{:S(2)}, u32[]{:S(2)}) collective-permute-start(f32[3,1,16,128]{3,2,0,1:T(8,128)S(1)} %get-tuple-element.900), channel_id=1, source_target_pairs={{8,0},{16,8},{24,16},{32,24},{40,32},{48,40},{56,48},{64,56},{72,6... | collective-permute-start | bytes 73736 | tf_op jit(solution)/shard_map/ppermute | solution.py:19
  29.9 4.2 collective-permute-start.6
  30.3 6.2 %collective-permute-start.7 = (f32[3,34,1,128]{3,2,0,1:T(1,128)S(1)}, f32[3,34,1,128]{3,2,0,1:T(1,128)S(1)}, u32[]{:S(2)}, u32[]{:S(2)}) collective-permute-start(f32[3,34,1,128]{3,2,0,1:T(1,128)S(1)} %get-tuple-element.891), channel_id=1, source_target_pairs={{0,1},{1,2},{2,3},{3,4},{4,5},{5,6},{6,7},{7,0},{8,9},{9,10},{10,1... | collective-permute-start | bytes 156680 | tf_op jit(solution)/shard_map/ppermute | solution.py:16
  32.1 7.8 %copy-start.4 = (f32[32,16,128]{2,1,0:T(8,128)}, f32[32,16,128]{2,1,0:T(8,128)S(1)}, u32[]{:S(2)}) copy-start(f32[32,16,128]{2,1,0:T(8,128)S(1)} %get-tuple-element.897) | copy-start | bytes 786436
  32.1 7.8 %copy-start.6 = (f32[32,16,128]{2,1,0:T(8,128)}, f32[32,16,128]{2,1,0:T(8,128)S(1)}, u32[]{:S(2)}) copy-start(f32[32,16,128]{2,1,0:T(8,128)S(1)} %get-tuple-element.898) | copy-start | bytes 786436
  36.5 3.4 copy-start.10
  39.9 73.0 %all-to-all-start = ((f32[3,3,32,16,128]{4,3,1,0,2:T(8,128)}), f32[3,3,32,16,128]{4,3,1,0,2:T(8,128)S(1)}, u32[]{:S(2)}, u32[]{:S(2)}) async-start(f32[3,3,32,16,128]{4,3,1,0,2:T(8,128)} %pad_maximum_fusion.1), calls=%async_computation | async-start | bytes 4718592 | tf_op jit(solution)/shard_map/all_to_all | solution.py:80
  55.5 28.2 %copy-start.1 = (f32[32,3,4,128,128]{4,0,3,2,1:T(8,128)}, f32[32,3,4,128,128]{4,0,3,2,1:T(8,128)S(1)}, u32[]{:S(2)}) copy-start(f32[32,3,4,128,128]{4,0,3,2,1:T(8,128)S(1)} %convert_multiply_fusion) | copy-start | bytes 75497472
  83.6 25.1 %copy-start.2 = (f32[35,32]{0,1:T(8,128)S(1)}, f32[35,32]{0,1:T(8,128)}, u32[]{:S(2)}) copy-start(f32[35,32]{0,1:T(8,128)} %param.149) | copy-start | bytes 13444
  83.6 27.3 %copy-start.5 = (f32[32,16,128]{2,1,0:T(8,128)S(1)}, f32[32,16,128]{2,1,0:T(8,128)}, u32[]{:S(2)}) copy-start(f32[32,16,128]{2,1,0:T(8,128)} %copy-done.4) | copy-start | bytes 786436
  83.7 27.3 %copy-start.7 = (f32[32,16,128]{2,1,0:T(8,128)S(1)}, f32[32,16,128]{2,1,0:T(8,128)}, u32[]{:S(2)}) copy-start(f32[32,16,128]{2,1,0:T(8,128)} %copy-done.6) | copy-start | bytes 786436
  83.7 27.2 %copy-start.8 = (f32[32,16,128]{2,1,0:T(8,128)S(1)}, f32[32,16,128]{2,1,0:T(8,128)}, u32[]{:S(2)}) copy-start(f32[32,16,128]{2,1,0:T(8,128)} %param.146) | copy-start | bytes 786436
  83.7 27.2 %copy-start.11 = (f32[3,34,1,128]{3,2,0,1:T(1,128)S(1)}, f32[3,34,1,128]{3,2,0,1:T(1,128)}, u32[]{:S(2)}) copy-start(f32[3,34,1,128]{3,2,0,1:T(1,128)} %copy-done.10) | copy-start | bytes 156676
  111.8 215.7 %copy-start.35 = (f32[32]{0:T(128)S(1)}, f32[32]{0:T(128)}, u32[]{:S(2)}) copy-start(f32[32]{0:T(128)} %get-tuple-element.889) | copy-start | bytes 388
  111.8 216.6 %copy-start.30 = (f32[32]{0:T(128)S(1)}, f32[32]{0:T(128)}, u32[]{:S(2)}) copy-start(f32[32]{0:T(128)} %get-tuple-element.888) | copy-start | bytes 388
  111.8 218.1 %copy-start.29 = (f32[32]{0:T(128)S(1)}, f32[32]{0:T(128)}, u32[]{:S(2)}) copy-start(f32[32]{0:T(128)} %get-tuple-element.887) | copy-start | bytes 388
  111.8 219.8 %copy-start.34 = (f32[32]{0:T(128)S(1)}, f32[32]{0:T(128)}, u32[]{:S(2)}) copy-start(f32[32]{0:T(128)} %get-tuple-element.886) | copy-start | bytes 388
  111.8 221.5 %copy-start.28 = (f32[32]{0:T(128)S(1)}, f32[32]{0:T(128)}, u32[]{:S(2)}) copy-start(f32[32]{0:T(128)} %get-tuple-element.885) | copy-start | bytes 388
  111.8 223.2 %copy-start.27 = (f32[32]{0:T(128)S(1)}, f32[32]{0:T(128)}, u32[]{:S(2)}) copy-start(f32[32]{0:T(128)} %get-tuple-element.884) | copy-start | bytes 388
  111.8 224.8 %copy-start.26 = (f32[32]{0:T(128)S(1)}, f32[32]{0:T(128)}, u32[]{:S(2)}) copy-start(f32[32]{0:T(128)} %get-tuple-element.883) | copy-start | bytes 388
  111.8 226.5 %copy-start.25 = (f32[32]{0:T(128)S(1)}, f32[32]{0:T(128)}, u32[]{:S(2)}) copy-start(f32[32]{0:T(128)} %get-tuple-element.882) | copy-start | bytes 388
  111.8 228.2 %copy-start.24 = (f32[32]{0:T(128)S(1)}, f32[32]{0:T(128)}, u32[]{:S(2)}) copy-start(f32[32]{0:T(128)} %get-tuple-element.881) | copy-start | bytes 388
  111.9 230.0 %copy-start.23 = (f32[32]{0:T(128)S(1)}, f32[32]{0:T(128)}, u32[]{:S(2)}) copy-start(f32[32]{0:T(128)} %get-tuple-element.880) | copy-start | bytes 388
  111.9 231.7 %copy-start.22 = (f32[32]{0:T(128)S(1)}, f32[32]{0:T(128)}, u32[]{:S(2)}) copy-start(f32[32]{0:T(128)} %get-tuple-element.879) | copy-start | bytes 388
  111.9 233.3 %copy-start.33 = (f32[32]{0:T(128)S(1)}, f32[32]{0:T(128)}, u32[]{:S(2)}) copy-start(f32[32]{0:T(128)} %get-tuple-element.878) | copy-start | bytes 388
  111.9 235.0 %copy-start.21 = (f32[32]{0:T(128)S(1)}, f32[32]{0:T(128)}, u32[]{:S(2)}) copy-start(f32[32]{0:T(128)} %get-tuple-element.877) | copy-start | bytes 388
  111.9 236.6 %copy-start.20 = (f32[32]{0:T(128)S(1)}, f32[32]{0:T(128)}, u32[]{:S(2)}) copy-start(f32[32]{0:T(128)} %get-tuple-element.876) | copy-start | bytes 388
  111.9 238.3 %copy-start.19 = (f32[32]{0:T(128)S(1)}, f32[32]{0:T(128)}, u32[]{:S(2)}) copy-start(f32[32]{0:T(128)} %get-tuple-element.875) | copy-start | bytes 388
  111.9 240.0 %copy-start.18 = (f32[32]{0:T(128)S(1)}, f32[32]{0:T(128)}, u32[]{:S(2)}) copy-start(f32[32]{0:T(128)} %get-tuple-element.873) | copy-start | bytes 388
  111.9 241.7 %copy-start.17 = (f32[32]{0:T(128)S(1)}, f32[32]{0:T(128)}, u32[]{:S(2)}) copy-start(f32[32]{0:T(128)} %get-tuple-element.872) | copy-start | bytes 388
  111.9 243.3 %copy-start.16 = (f32[32]{0:T(128)S(1)}, f32[32]{0:T(128)}, u32[]{:S(2)}) copy-start(f32[32]{0:T(128)} %get-tuple-element.871) | copy-start | bytes 388
  111.9 245.0 %copy-start.15 = (f32[32]{0:T(128)S(1)}, f32[32]{0:T(128)}, u32[]{:S(2)}) copy-start(f32[32]{0:T(128)} %get-tuple-element.870) | copy-start | bytes 388
  112.0 246.7 %copy-start.32 = (f32[32]{0:T(128)S(1)}, f32[32]{0:T(128)}, u32[]{:S(2)}) copy-start(f32[32]{0:T(128)} %get-tuple-element.869) | copy-start | bytes 388
  112.0 248.3 %copy-start.14 = (f32[32]{0:T(128)S(1)}, f32[32]{0:T(128)}, u32[]{:S(2)}) copy-start(f32[32]{0:T(128)} %get-tuple-element.868) | copy-start | bytes 388
  112.0 250.0 %copy-start.13 = (f32[32]{0:T(128)S(1)}, f32[32]{0:T(128)}, u32[]{:S(2)}) copy-start(f32[32]{0:T(128)} %get-tuple-element.867) | copy-start | bytes 388
  112.0 251.6 %copy-start.12 = (f32[32]{0:T(128)S(1)}, f32[32]{0:T(128)}, u32[]{:S(2)}) copy-start(f32[32]{0:T(128)} %get-tuple-element.866) | copy-start | bytes 388
  112.0 260.2 %copy-start.31 = (f32[32]{0:T(128)S(1)}, f32[32]{0:T(128)}, u32[]{:S(2)}) copy-start(f32[32]{0:T(128)} %get-tuple-element.861) | copy-start | bytes 388
  113.0 1.4 copy-start.3
  245.7 2.1 copy-start.9
  325.4 4.4 copy-start
